TPU v7x, 128 devices: a whole 4x4x4 slice. The times are simulated.
128 devices in a mesh: grp: 4 (over y), col: 32 (over x, z, core).
Axes of the slice: x: 4, y: 4, z: 4, core: 2. Of those that a mesh axis runs over, the one named last changes fastest.
Arguments:
- blocks: bfloat16 [24576, 32, 1024], P(('grp', 'col'))
- i_index: int32 [24576], P(('grp', 'col')), may hold values from 0 to 63
- j_index: int32 [24576], P(('grp', 'col')), may hold values from 0 to 63
- k_index: int32 [24576], P(('grp', 'col')), may hold values from 0 to 15
- block_count: int32 [128], P(('grp', 'col')), may hold values from 24 to 192, as said below
- b_factor: float32 [65536, 256], P(('grp', 'col'))
- c_factor: float32 [16384, 256], P(('grp', 'col'))
Outputs:
- a_update: float32 [8192, 256], P(('grp', 'col'))
- b_update: float32 [65536, 256], P(('grp', 'col'))
Inputs may be any that keep to these rules, and one draw needn't show every extreme that they name: block_count[d] is the number of live slots of device d = 32 * (grp index) + (col index): its slots d * 192 to d * 192 + block_count[d] - 1; every other slot is ignored. Some device has exactly 192 live slots.
All inputs are finite; a program needn't handle non-finite values.
Results may differ from a plain program's by a relative error of at most 0.005.
The roundings to bfloat16 on the way count: a program that leaves them out, or rounds other values in their place, can miss the bound.
Values may be sent and summed in bfloat16 or wider, within the bound.
No kernel may reach another device: no remote copies, remote signals or barrier semaphores. Data moves between devices by JAX's collectives and lax.ppermute only.
A program may use at most 128 MiB of HBM per device.

v0:
```python
import jax
import jax.numpy as jnp
from jax import lax
from jax.sharding import PartitionSpec as P

A_DEV = 2


def solve_rows(gram, right_side):
    factor_low = lax.linalg.cholesky(gram)
    halfway = lax.linalg.triangular_solve(
        factor_low, right_side, left_side=False, lower=True, transpose_a=True
    )
    return lax.linalg.triangular_solve(
        factor_low, halfway, left_side=False, lower=True, transpose_a=False
    )


def mode_term(
    blocks,
    left_rows,
    left_index,
    tail_rows,
    tail_index,
    target_index,
    live_mask,
    targets,
    first_mode,
):
    block_edge = blocks.shape[1]
    rank_width = left_rows.shape[1]
    group_size = 16
    groups = blocks.shape[0] // group_size
    left_table = left_rows.reshape(-1, block_edge, rank_width)
    tail_table = tail_rows.reshape(-1, block_edge, rank_width)
    target_ids = jnp.arange(targets, dtype=jnp.int32)

    def one_step(running, inputs):
        tensor_group, left_idx, tail_idx, target_idx, alive_row = inputs
        left_blk = left_table[left_idx].astype(jnp.float32)
        tail_blk = tail_table[tail_idx].astype(jnp.float32)
        product = (left_blk[:, :, None, :] * tail_blk[:, None, :, :]).astype(jnp.bfloat16)
        if first_mode:
            result = jnp.einsum(
                "bim,bmr->bir",
                tensor_group,
                product.reshape(group_size, block_edge * block_edge, rank_width),
                preferred_element_type=jnp.float32,
            )
        else:
            result = jnp.einsum(
                "bijk,bikr->bjr",
                tensor_group.reshape(group_size, block_edge, block_edge, block_edge),
                product,
                preferred_element_type=jnp.float32,
            )
        select = (target_idx[None, :] == target_ids[:, None]).astype(jnp.float32) * alive_row[
            None, :
        ]
        update = jnp.dot(
            select,
            result.reshape(group_size, block_edge * rank_width),
            precision=lax.Precision.HIGHEST,
        )
        return (running + update, None)

    inputs = (
        blocks.reshape(groups, group_size, block_edge, block_edge * block_edge),
        left_index.reshape(groups, group_size),
        tail_index.reshape(groups, group_size),
        target_index.reshape(groups, group_size),
        live_mask.reshape(groups, group_size),
    )
    start_value = jnp.zeros((targets, block_edge * rank_width), jnp.float32)
    running, _ = lax.scan(one_step, start_value, inputs)
    return running.reshape(targets * block_edge, rank_width)


def on_device(blocks, i_index, j_index, k_index, block_count, b_factor, c_factor):
    highest = lax.Precision.HIGHEST
    block_edge = blocks.shape[1]
    gram_second, gram_third = lax.psum(
        (
            jnp.dot(b_factor.T, b_factor, precision=highest),
            jnp.dot(c_factor.T, c_factor, precision=highest),
        ),
        ("grp", "col"),
    )
    b_range, c_range = (
        lax.all_gather(b_factor.astype(jnp.bfloat16), "grp", axis=0, tiled=True),
        lax.all_gather(c_factor.astype(jnp.bfloat16), "grp", axis=0, tiled=True),
    )
    live_mask = (jnp.arange(blocks.shape[0], dtype=jnp.int32) < block_count[0]).astype(jnp.float32)
    first_targets = A_DEV * lax.axis_size("col")
    second_targets = b_range.shape[0] // block_edge
    partial_value = mode_term(
        blocks, b_range, j_index, c_range, k_index, i_index, live_mask, first_targets, True
    )
    gram_one = gram_second * gram_third
    whole_sum = lax.psum(partial_value, "col")
    a_whole = solve_rows(gram_one, whole_sum)
    gram_first = lax.psum(jnp.dot(a_whole.T, a_whole, precision=highest), "grp")
    col_norm = jnp.sqrt(jnp.diagonal(gram_first) + 1e-06)
    a_range = (a_whole / col_norm[None, :]).astype(jnp.bfloat16)
    own_rows = A_DEV * block_edge
    a_update = lax.dynamic_slice_in_dim(a_whole, lax.axis_index("col") * own_rows, own_rows, 0)
    gram_two = gram_first / (col_norm[:, None] * col_norm[None, :]) * gram_third
    partial_two = mode_term(
        blocks, a_range, i_index, c_range, k_index, j_index, live_mask, second_targets, False
    )
    own_two = lax.psum_scatter(partial_two, "grp", scatter_dimension=0, tiled=True)
    b_update = solve_rows(gram_two, own_two)
    return (a_update, b_update)


def solution(mesh):
    return jax.shard_map(
        on_device,
        mesh=mesh,
        in_specs=(
            P(("grp", "col"), None, None),
            P(("grp", "col")),
            P(("grp", "col")),
            P(("grp", "col")),
            P(("grp", "col")),
            P(("grp", "col"), None),
            P(("grp", "col"), None),
        ),
        out_specs=(P(("grp", "col"), None), P(("grp", "col"), None)),
        check_vma=False,
    )
```

profile of v0, /device:TPU:0, one launch (start us, length us, event | category | flops | bytes accessed | tf_op | source)
XLA Modules:
  0.0 780.1 jit_solution(10742429783290168959)
XLA Ops:
  15.0 13.0 %all_gather.7 = bf16[512,256]{1,0:T(8,128)(2,1)S(1)} all-gather(bf16[128,256]{1,0:T(8,128)(2,1)S(1)} %convert_element_type.56), channel_id=1, replica_groups=mesh['grp'=4,'col'=32] {'grp'}, dimensions={0}, use_global_device_ids=true | all-gather | bytes 327680 | tf_op jit(solution)/shard_map/all_gather | solution.py:91
  28.0 135.6 %all-reduce.10.cloned.1.call-done = (f32[256,256]{0,1:T(8,128)}, f32[256,256]{0,1:T(8,128)}) async-done(((f32[256,256]{0,1:T(8,128)}, f32[256,256]{0,1:T(8,128)}), (f32[256,256]{0,1:T(8,128)}, f32[256,256]{0,1:T(8,128)})) %all-reduce.10.cloned.1.call-update) | async-done | bytes 524304 | tf_op jit(solution)/shard_map/psum | solution.py:82
  164.8 11.7 %custom-call.29 = f32[128,128]{1,0:T(8,128)S(1)} custom-call(f32[128,128]{1,0:T(8,128)S(1)} %slice.101), custom_call_target="Cholesky" | custom-call | tf_op jit(solution)/shard_map/cholesky/custom-call.2 | solution.py:10
  176.6 9.8 %custom-call.30 = f32[1,128,128]{1,2,0:T(8,128)S(1)} custom-call(f32[1,128,128]{2,1,0:T(8,128)S(1)} %get-tuple-element.262), custom_call_target="InvertDiagBlocksLowerTriangular" | custom-call | tf_op jit(solution)/shard_map/cholesky/custom-call.7 | solution.py:10
  187.1 11.7 %custom-call.31 = f32[128,128]{1,0:T(8,128)S(1)} custom-call(f32[128,128]{1,0:T(8,128)S(1)} %convolution_subtract_fusion.5), custom_call_target="Cholesky" | custom-call | tf_op jit(solution)/shard_map/cholesky/custom-call.3 | solution.py:10
  198.9 141.3 %while.26 = (s32[]{:T(128)}, f32[64,8192]{1,0:T(8,128)S(1)}, s32[12,16]{1,0:T(8,128)S(1)}, f32[12,16]{1,0:T(8,128)S(1)}, bf16[12,16,32,1024]{3,2,1,0:T(8,128)(2,...) while((s32[]{:T(128)}, f32[64,8192]{1,0:T(8,128)S(1)}, ...), condition=%wide.region_1.0_spmd.clone, body=%wide.region_0.0_spmd.clone.sunk | while | flops 378802272 | bytes 27796492 | solution.py:75
  201.6 3.9 multiply_convert_fusion.5
  213.3 3.9 multiply_convert_fusion.5
  225.1 3.9 multiply_convert_fusion.5
  236.8 3.9 multiply_convert_fusion.5
  248.6 3.9 multiply_convert_fusion.5
  260.4 3.9 multiply_convert_fusion.5
  272.1 3.9 multiply_convert_fusion.5
  344.0 4.3 while.24
  348.3 19.7 %custom-call.20 = f32[2,128,128]{1,2,0:T(8,128)S(1)} custom-call(f32[2,128,128]{2,1,0:T(8,128)S(1)} %get-tuple-element.116), custom_call_target="InvertDiagBlocksLowerTriangular" | custom-call | tf_op jit(solution)/shard_map/triangular_solve | solution.py:11
  368.0 80.2 %all-reduce.6.cloned.1.call-done = f32[2048,256]{1,0:T(8,128)} async-done(((f32[2048,256]{1,0:T(8,128)}), f32[2048,256]{1,0:T(8,128)}) %all-reduce.6.cloned.1.call-update) | async-done | bytes 2097168 | tf_op jit(solution)/shard_map/psum | solution.py:100
  456.5 4.2 fusion.33
  461.2 40.8 %all-reduce.8.cloned.1.call-done = f32[256,256]{0,1:T(8,128)} async-done(((f32[256,256]{0,1:T(8,128)}), f32[256,256]{0,1:T(8,128)}) %all-reduce.8.cloned.1.call-update) | async-done | bytes 262160 | tf_op jit(solution)/shard_map/psum | solution.py:102
  507.1 195.0 %while.27 = (s32[]{:T(128)}, f32[64,8192]{1,0:T(8,128)S(1)}, s32[12,16]{1,0:T(8,128)}, f32[12,16]{1,0:T(8,128)}, bf16[12,16,32,1024]{3,2,1,0:T(8,128)(2,1)}, /*i...) while((s32[]{:T(128)}, f32[64,8192]{1,0:T(8,128)S(1)}, ...), condition=%wide.region_11.13_spmd.clone, body=%wide.region_10.12_spmd.clone.sunk | while | flops 378802272 | bytes 15213583 | solution.py:75
  508.4 4.4 reshape.345
  515.3 4.0 fusion.116
  524.7 4.4 reshape.345
  531.5 4.0 fusion.116
  540.9 4.4 reshape.345
  547.8 4.0 fusion.116
  557.2 4.4 reshape.345
  564.0 4.0 fusion.116
  573.4 4.4 reshape.345
  580.3 4.0 fusion.116
  589.7 4.4 reshape.345
  596.5 4.0 fusion.116
  605.9 4.4 reshape.345
  612.8 4.0 fusion.116
  622.2 4.4 reshape.345
  629.0 4.0 fusion.116
  638.4 4.4 reshape.345
  645.3 4.0 fusion.116
  654.7 4.4 reshape.345
  661.5 4.0 fusion.116
  670.9 4.4 reshape.345
  677.8 4.0 fusion.116
  687.2 4.4 reshape.345
  694.0 4.0 fusion.116
  706.2 11.7 %custom-call.32 = f32[128,128]{1,0:T(8,128)S(1)} custom-call(f32[128,128]{1,0:T(8,128)S(1)} %slice.104), custom_call_target="Cholesky" | custom-call | tf_op jit(solution)/shard_map/cholesky/custom-call.2 | solution.py:10
  718.0 9.8 %custom-call.33 = f32[1,128,128]{1,2,0:T(8,128)S(1)} custom-call(f32[1,128,128]{2,1,0:T(8,128)S(1)} %get-tuple-element.258), custom_call_target="InvertDiagBlocksLowerTriangular" | custom-call | tf_op jit(solution)/shard_map/cholesky/custom-call.7 | solution.py:10
  728.5 11.7 %custom-call.34 = f32[128,128]{1,0:T(8,128)S(1)} custom-call(f32[128,128]{1,0:T(8,128)S(1)} %convolution_subtract_fusion.4), custom_call_target="Cholesky" | custom-call | tf_op jit(solution)/shard_map/cholesky/custom-call.3 | solution.py:10
  742.9 4.0 while.25
  746.9 19.8 %custom-call.21 = f32[2,128,128]{1,2,0:T(8,128)S(1)} custom-call(f32[2,128,128]{2,1,0:T(8,128)S(1)} %get-tuple-element.124), custom_call_target="InvertDiagBlocksLowerTriangular" | custom-call | tf_op jit(solution)/shard_map/triangular_solve | solution.py:11
  (415 shorter events, 249.8 us)
Async XLA Ops:
  8.0 5.2 copy-start.5
  8.0 6.0 copy-start.8
  8.0 6.0 copy-start.12
  8.0 6.8 copy-start.13
  8.0 6.9 copy-start.14
  8.0 155.5 %all-reduce.10.cloned.1.call-start = ((), (), s32[]{:S(2)}) async-start(), calls=%async_computation.5 | async-start | bytes 1048576 | tf_op jit(solution)/shard_map/psum | solution.py:82
  13.2 185.7 %all-gather.2.cloned.1.call-start = ((), (), s32[]{:S(2)}) async-start(), calls=%async_computation.1 | async-start | bytes 1310720 | tf_op jit(solution)/shard_map/all_gather | solution.py:90
  14.0 434.3 %all-reduce.6.cloned.1.call-start = ((), (), s32[]{:S(2)}) async-start(), calls=%async_computation.2 | async-start | bytes 4194304 | tf_op jit(solution)/shard_map/psum | solution.py:100
  340.2 1.5 copy-start.10
  340.2 1.5 copy-start.11
  341.8 160.2 %all-reduce.8.cloned.1.call-start = ((), (), s32[]{:S(2)}) async-start(), calls=%async_computation.3 | async-start | bytes 524288 | tf_op jit(solution)/shard_map/psum | solution.py:102
  348.3 103.3 %copy-start.7 = (f32[256,256]{1,0:T(8,128)}, f32[256,256]{1,0:T(8,128)S(1)}, u32[]{:S(2)}) copy-start(f32[256,256]{1,0:T(8,128)S(1)} %get-tuple-element.553) | copy-start | bytes 786436
  348.3 103.3 %copy-start.15 = (s32[2,2]{1,0:T(2,128)}, s32[2,2]{1,0:T(2,128)S(1)}, u32[]{:S(2)}) copy-start(s32[2,2]{1,0:T(2,128)S(1)} %get-tuple-element.571) | copy-start | bytes 52
  448.3 2.4 copy-start.6
  453.6 51.0 %copy-start = (f32[2048,128]{1,0:T(8,128)}, f32[2048,128]{1,0:T(8,128)S(1)}, u32[]{:S(2)}) copy-start(f32[2048,128]{1,0:T(8,128)S(1)} %fusion.48) | copy-start | bytes 3145732
  456.5 4.7 copy-start.2
  460.7 306.1 %reduce-scatter.2.cloned.1.call-start = ((), (), s32[]{:S(2)}) async-start(), calls=%async_computation.4 | async-start | bytes 2621440 | tf_op jit(solution)/shard_map/reduce_scatter | solution.py:111
  703.6 1.2 copy-start.1
  703.6 1.5 copy-start.3
  703.6 2.2 copy-start.4
  703.6 2.2 copy-start.9
  706.0 36.9 %copy-start.16 = (s32[2,2]{1,0:T(2,128)S(1)}, s32[2,2]{1,0:T(2,128)}, u32[]{:S(2)}) copy-start(s32[2,2]{1,0:T(2,128)} %copy-done.15) | copy-start | bytes 52
Sparse Core Ops, SparseCore 0:
  13.8 149.6 all-reduce.9
Sparse Core Ops, SparseCore 1:
  15.9 26.6 all-gather.1
  341.9 106.3 all-reduce.5
  460.8 41.2 all-reduce.7
  703.7 30.0 reduce-scatter.1
where the time goes:
time: 792 us; the launch traced here: 780 us
  waiting for transfers between devices  257 us (32%)
  local copies, waits for them, and re-layouts  166 us (21%)
  other arithmetic  162 us (20%)
  matrix products  159 us (20%)
  between operations  19.7 us (2%)
  blocking collectives  13 us (2%)
    psum x1, waiting for transfers between devices, on_device(): lax.psum((jnp.dot(b_factor.T, b_factor, precision=highest), jnp.dot(c_fac...  136 us
    psum x1, waiting for transfers between devices, on_device(): whole_sum = lax.psum(partial_value, 'col')  80.2 us
    another operation x13, other arithmetic, solve_rows(): factor_low = lax.linalg.cholesky(gram)  68.6 us
    dot_general x24, matrix products, one_step(): jnp.dot(select, result.reshape(group_size, block_edge * rank_width), prec...  55 us
    reshape x12, local copies, waits for them, and re-layouts, one_step(): tensor_group.reshape(group_size, block_edge, block_edge, block_edge)  52.3 us
    dot_general x12, matrix products, one_step(): jnp.einsum('bijk,bikr->bjr', tensor_group.reshape(group_size, block_edge,...  48.5 us
    convert_element_type x12, other arithmetic, one_step(): (left_blk[:, :, None, :] * tail_blk[:, None, :, :]).astype(jnp.bfloat16)  46.2 us
    gather x24, local copies, waits for them, and re-layouts, one_step(): left_blk = left_table[left_idx].astype(jnp.float32)  42.9 us
  transfers between devices with their start and end apart: 5, of which 3 were waited for; matrix products, arithmetic and copies ran while one was open for 15% of the time, Pallas kernels for 0%

commit v1 on v0

--- a/solution.py
+++ b/solution.py
@@ -79,12 +79,15 @@
 def on_device(blocks, i_index, j_index, k_index, block_count, b_factor, c_factor):
     highest = lax.Precision.HIGHEST
     block_edge = blocks.shape[1]
-    gram_second, gram_third = lax.psum(
-        (
-            jnp.dot(b_factor.T, b_factor, precision=highest),
-            jnp.dot(c_factor.T, c_factor, precision=highest),
+    gram_second, gram_third = jax.lax.psum(
+        jax.lax.psum(
+            (
+                jnp.dot(b_factor.T, b_factor, precision=highest),
+                jnp.dot(c_factor.T, c_factor, precision=highest),
+            ),
+            axis_name="grp",
         ),
-        ("grp", "col"),
+        "col",
     )
     b_range, c_range = (
         lax.all_gather(b_factor.astype(jnp.bfloat16), "grp", axis=0, tiled=True),

time: 792 us -> 711 us (0.90)
  waiting for transfers between devices: 257 us -> 161 us
  other arithmetic: 162 us -> 182 us
    psum x1, waiting for transfers between devices: 136 us -> 0.01 us  [on_device(): jax.lax.psum((jnp.dot(b_factor.T, b_factor, precision=highest), jnp.dot(c...]
    psum x1, waiting for transfers between devices: 80.2 us -> 110 us  [on_device(): whole_sum = lax.psum(partial_value, 'col')]
    all_gather x1, waiting for transfers between devices: 0.03 us -> 9.89 us  [on_device(): lax.all_gather(b_factor.astype(jnp.bfloat16), 'grp', axis=0, tiled=True)]
    convert_element_type x24, other arithmetic: 0.97 us -> 10.6 us  [one_step(): tail_blk = tail_table[tail_idx].astype(jnp.float32)]
    convert_element_type x24, other arithmetic: 0.97 us -> 10.6 us  [one_step(): left_blk = left_table[left_idx].astype(jnp.float32)]
  transfers between devices with their start and end apart: 5 -> 5, of which waited for: 3 -> 3; matrix products, arithmetic and copies ran while one was open for 15% -> 29% of each run, Pallas kernels for 0% -> 0%
where the time goes in v1:
time: 711 us; the launch traced here: 702 us
  other arithmetic  182 us (26%)
  local copies, waits for them, and re-layouts  167 us (23%)
  waiting for transfers between devices  161 us (23%)
  matrix products  158 us (22%)
  between operations  17.7 us (2%)
  blocking collectives  12.9 us (2%)
    psum x1, waiting for transfers between devices, on_device(): whole_sum = lax.psum(partial_value, 'col')  110 us
    another operation x13, other arithmetic, solve_rows(): factor_low = lax.linalg.cholesky(gram)  68.6 us
    dot_general x24, matrix products, one_step(): jnp.dot(select, result.reshape(group_size, block_edge * rank_width), prec...  54.9 us
    reshape x12, local copies, waits for them, and re-layouts, one_step(): tensor_group.reshape(group_size, block_edge, block_edge, block_edge)  52.3 us
    dot_general x12, matrix products, one_step(): jnp.einsum('bijk,bikr->bjr', tensor_group.reshape(group_size, block_edge,...  51.1 us
    convert_element_type x12, other arithmetic, one_step(): (left_blk[:, :, None, :] * tail_blk[:, None, :, :]).astype(jnp.bfloat16)  46.2 us
    gather x24, local copies, waits for them, and re-layouts, one_step(): left_blk = left_table[left_idx].astype(jnp.float32)  42.9 us
    psum x1, waiting for transfers between devices, on_device(): gram_first = lax.psum(jnp.dot(a_whole.T, a_whole, precision=highest), 'grp')  41.1 us
  transfers between devices with their start and end apart: 5, of which 3 were waited for; matrix products, arithmetic and copies ran while one was open for 29% of the time, Pallas kernels for 0%

profile of v1, /device:TPU:0, one launch (start us, length us, event | category | flops | bytes accessed | tf_op | source)
XLA Modules:
  0.0 701.8 jit_solution(14878679305588226521)
XLA Ops:
  13.1 12.9 %all_gather.7 = bf16[512,256]{1,0:T(8,128)(2,1)S(1)} all-gather(bf16[128,256]{1,0:T(8,128)(2,1)S(1)} %convert_element_type.56), channel_id=1, replica_groups=mesh['grp'=4,'col'=32] {'grp'}, dimensions={0}, use_global_device_ids=true | all-gather | bytes 327680 | tf_op jit(solution)/shard_map/all_gather | solution.py:94
  26.9 9.9 %all-gather.2.cloned.1.call-done = bf16[2048,256]{1,0:T(8,128)(2,1)} async-done(((bf16[512,256]{1,0:T(8,128)(2,1)}), bf16[2048,256]{1,0:T(8,128)(2,1)}) %all-gather.2.cloned.1.call-update) | async-done | bytes 1048592 | tf_op jit(solution)/shard_map/all_gather | solution.py:93
  36.8 141.0 %while.26 = (s32[]{:T(128)}, f32[64,8192]{1,0:T(8,128)S(1)}, s32[12,16]{1,0:T(8,128)S(1)}, f32[12,16]{1,0:T(8,128)S(1)}, bf16[12,16,32,1024]{3,2,1,0:T(8,128)(2,...) while((s32[]{:T(128)}, f32[64,8192]{1,0:T(8,128)S(1)}, ...), condition=%wide.region_1.0_spmd.clone, body=%wide.region_0.0_spmd.clone.sunk | while | flops 378802272 | bytes 27796992 | solution.py:75
  39.3 3.9 multiply_convert_fusion.5
  51.0 3.9 multiply_convert_fusion.5
  62.8 3.9 multiply_convert_fusion.5
  74.5 3.9 multiply_convert_fusion.5
  86.3 3.9 multiply_convert_fusion.5
  98.1 3.9 multiply_convert_fusion.5
  109.8 3.9 multiply_convert_fusion.5
  121.6 3.9 multiply_convert_fusion.5
  179.6 109.8 %all-reduce.9.cloned.1.call-done = (f32[2048,256]{1,0:T(8,128)}, f32[256,256]{0,1:T(8,128)}, f32[256,256]{0,1:T(8,128)}) async-done(((f32[2048,256]{1,0:T(8,128)}, f32[256,256]{0,1:T(8,128)}, f32[256,256]{0,1:T(8,128)}), (f32[2048,256]{1,0:T(8,128)}, f32[256,256]{0,1:T(8,128)}, f32[256,256]{0,1:T(8,128)})) %all-reduce.9.cloned.1.call-update) | async-done | bytes 2621456 | tf_op jit(solution)/shard_map/psum | solution.py:103
  290.8 11.7 %custom-call.29 = f32[128,128]{1,0:T(8,128)S(1)} custom-call(f32[128,128]{1,0:T(8,128)S(1)} %slice.101), custom_call_target="Cholesky" | custom-call | tf_op jit(solution)/shard_map/cholesky/custom-call.2 | solution.py:10
  302.5 9.8 %custom-call.30 = f32[1,128,128]{1,2,0:T(8,128)S(1)} custom-call(f32[1,128,128]{2,1,0:T(8,128)S(1)} %get-tuple-element.265), custom_call_target="InvertDiagBlocksLowerTriangular" | custom-call | tf_op jit(solution)/shard_map/cholesky/custom-call.7 | solution.py:10
  313.0 11.7 %custom-call.31 = f32[128,128]{1,0:T(8,128)S(1)} custom-call(f32[128,128]{1,0:T(8,128)S(1)} %convolution_subtract_fusion.5), custom_call_target="Cholesky" | custom-call | tf_op jit(solution)/shard_map/cholesky/custom-call.3 | solution.py:10
  326.9 4.5 while.24
  331.3 19.7 %custom-call.20 = f32[2,128,128]{1,2,0:T(8,128)S(1)} custom-call(f32[2,128,128]{2,1,0:T(8,128)S(1)} %get-tuple-element.116), custom_call_target="InvertDiagBlocksLowerTriangular" | custom-call | tf_op jit(solution)/shard_map/triangular_solve | solution.py:11
  357.9 4.2 fusion.33
  362.4 41.1 %all-reduce.7.cloned.1.call-done = f32[256,256]{0,1:T(8,128)} async-done(((f32[256,256]{0,1:T(8,128)}), f32[256,256]{0,1:T(8,128)}) %all-reduce.7.cloned.1.call-update) | async-done | bytes 262160 | tf_op jit(solution)/shard_map/psum | solution.py:105
  408.7 216.4 %while.27 = (s32[]{:T(128)}, f32[64,8192]{1,0:T(8,128)S(1)}, s32[12,16]{1,0:T(8,128)}, f32[12,16]{1,0:T(8,128)}, bf16[12,16,32,1024]{3,2,1,0:T(8,128)(2,1)}, /*i...) while((s32[]{:T(128)}, f32[64,8192]{1,0:T(8,128)S(1)}, ...), condition=%wide.region_13.15_spmd.clone, body=%wide.region_12.14_spmd.clone.sunk | while | flops 378802272 | bytes 15213575 | solution.py:75
  414.1 4.4 reshape.345
  418.4 4.3 fusion.116
  432.1 4.4 reshape.345
  436.5 4.3 fusion.116
  450.1 4.4 reshape.345
  454.5 4.3 fusion.116
  468.2 4.4 reshape.345
  472.5 4.3 fusion.116
  486.2 4.4 reshape.345
  490.5 4.3 fusion.116
  504.2 4.4 reshape.345
  508.6 4.3 fusion.116
  522.2 4.4 reshape.345
  526.6 4.3 fusion.116
  540.3 4.4 reshape.345
  544.6 4.3 fusion.116
  558.3 4.4 reshape.345
  562.7 4.3 fusion.116
  576.3 4.4 reshape.345
  580.7 4.3 fusion.116
  594.4 4.4 reshape.345
  598.8 4.3 fusion.116
  612.4 4.4 reshape.345
  616.8 4.3 fusion.116
  629.2 11.7 %custom-call.32 = f32[128,128]{1,0:T(8,128)S(1)} custom-call(f32[128,128]{1,0:T(8,128)S(1)} %slice.104), custom_call_target="Cholesky" | custom-call | tf_op jit(solution)/shard_map/cholesky/custom-call.2 | solution.py:10
  641.0 9.8 %custom-call.33 = f32[1,128,128]{1,2,0:T(8,128)S(1)} custom-call(f32[1,128,128]{2,1,0:T(8,128)S(1)} %get-tuple-element.261), custom_call_target="InvertDiagBlocksLowerTriangular" | custom-call | tf_op jit(solution)/shard_map/cholesky/custom-call.7 | solution.py:10
  651.5 11.7 %custom-call.34 = f32[128,128]{1,0:T(8,128)S(1)} custom-call(f32[128,128]{1,0:T(8,128)S(1)} %convolution_subtract_fusion.4), custom_call_target="Cholesky" | custom-call | tf_op jit(solution)/shard_map/cholesky/custom-call.3 | solution.py:10
  669.7 19.9 %custom-call.21 = f32[2,128,128]{1,2,0:T(8,128)S(1)} custom-call(f32[2,128,128]{2,1,0:T(8,128)S(1)} %get-tuple-element.124), custom_call_target="InvertDiagBlocksLowerTriangular" | custom-call | tf_op jit(solution)/shard_map/triangular_solve | solution.py:11
  (413 shorter events, 267.1 us)
Async XLA Ops:
  7.2 4.1 copy-start.5
  7.2 5.9 copy-start.7
  7.2 19.4 %copy-start.11 = (s32[192]{0:T(256)S(1)}, s32[192]{0:T(256)}, u32[]{:S(2)}) copy-start(s32[192]{0:T(256)} %param.13) | copy-start | bytes 2308
  7.2 19.5 %copy-start.12 = (s32[192]{0:T(256)S(1)}, s32[192]{0:T(256)}, u32[]{:S(2)}) copy-start(s32[192]{0:T(256)} %param.14) | copy-start | bytes 2308
  7.2 19.6 %copy-start.13 = (s32[192]{0:T(256)S(1)}, s32[192]{0:T(256)}, u32[]{:S(2)}) copy-start(s32[192]{0:T(256)} %param.15) | copy-start | bytes 2308
  7.2 29.6 %all-gather.2.cloned.1.call-start = ((), (), s32[]{:S(2)}) async-start(), calls=%async_computation.1 | async-start | bytes 1310720 | tf_op jit(solution)/shard_map/all_gather | solution.py:93
  9.1 170.3 %all-reduce.11.cloned.1.call-start = ((), (), s32[]{:S(2)}) async-start(), calls=%async_computation.5 | async-start | bytes 1048576 | tf_op jit(solution)/shard_map/psum | solution.py:83
  13.0 276.5 %all-reduce.9.cloned.1.call-start = ((), (), s32[]{:S(2)}) async-start(), calls=%async_computation.4 | async-start | bytes 5242880 | tf_op jit(solution)/shard_map/psum | solution.py:103
  177.8 1.5 copy-start.9
  177.8 1.5 copy-start.10
  179.4 224.2 %all-reduce.7.cloned.1.call-start = ((), (), s32[]{:S(2)}) async-start(), calls=%async_computation.2 | async-start | bytes 524288 | tf_op jit(solution)/shard_map/psum | solution.py:105
  290.6 60.5 %copy-start.6 = (f32[2048,256]{1,0:T(8,128)S(1)}, f32[2048,256]{1,0:T(8,128)}, u32[]{:S(2)}) copy-start(f32[2048,256]{1,0:T(8,128)} %get-tuple-element.245) | copy-start | bytes 6291460
  331.3 21.7 %copy-start.14 = (s32[2,2]{1,0:T(2,128)}, s32[2,2]{1,0:T(2,128)S(1)}, u32[]{:S(2)}) copy-start(s32[2,2]{1,0:T(2,128)S(1)} %get-tuple-element.584) | copy-start | bytes 52
  355.0 51.2 %copy-start = (f32[2048,128]{1,0:T(8,128)}, f32[2048,128]{1,0:T(8,128)S(1)}, u32[]{:S(2)}) copy-start(f32[2048,128]{1,0:T(8,128)S(1)} %fusion.48) | copy-start | bytes 3145732
  357.0 1.0 copy-start.2
  362.2 327.4 %reduce-scatter.2.cloned.1.call-start = ((), (), s32[]{:S(2)}) async-start(), calls=%async_computation.3 | async-start | bytes 2621440 | tf_op jit(solution)/shard_map/reduce_scatter | solution.py:114
  626.6 1.2 copy-start.1
  626.6 1.5 copy-start.3
  626.6 2.2 copy-start.4
  626.6 2.2 copy-start.8
  629.0 36.8 %copy-start.15 = (s32[2,2]{1,0:T(2,128)S(1)}, s32[2,2]{1,0:T(2,128)}, u32[]{:S(2)}) copy-start(s32[2,2]{1,0:T(2,128)} %copy-done.14) | copy-start | bytes 52
Sparse Core Ops, SparseCore 0:
  10.3 26.4 all-gather.1
  39.2 43.8 all-reduce.10
  179.5 109.9 all-reduce.8
  362.3 41.2 all-reduce.6
  626.7 30.1 reduce-scatter.1
